TPU v7x, 32 devices: a whole 2x2x4 slice. The times are simulated.
32 devices in a mesh: groups: 2 (over y), seq: 8 (over z, x), tp: 2 (over core).
Axes of the slice: x: 2, y: 2, z: 4, core: 2. Of those that a mesh axis runs over, the one named last changes fastest.
Arguments:
- span_queries: bfloat16 [128, 64, 128], P(('groups', 'seq'), 'tp'), parts along dimension 0, may hold values from -180 to 180
- span_keys: bfloat16 [128, 4, 128], P(('groups', 'seq'), 'tp'), parts along dimension 0, may hold values from -9 to 9
- span_values: bfloat16 [128, 4, 128], P(('groups', 'seq'), 'tp'), parts along dimension 0, may hold values from -6.5 to 6.5
- prefix_keys: bfloat16 [1152, 4, 128], P(('groups', 'seq'), 'tp'), parts along dimension 0, may hold values from -9 to 9
- prefix_values: bfloat16 [1152, 4, 128], P(('groups', 'seq'), 'tp'), parts along dimension 0, may hold values from -6.5 to 6.5
- prefix_lengths: int32 [16], P('groups'), parts along dimension 0, may hold values from 1 to 72
- decode_queries: bfloat16 [32, 64, 128], P(('groups', 'seq'), 'tp'), parts along dimension 0, may hold values from -180 to 180
- decode_new_keys: bfloat16 [32, 4, 128], P(('groups', 'seq'), 'tp'), parts along dimension 0, may hold values from -6 to 6
- decode_new_values: bfloat16 [32, 4, 128], P(('groups', 'seq'), 'tp'), parts along dimension 0, may hold values from -6 to 6
- decode_key_cache: bfloat16 [64, 256, 4, 128], P(('groups', 'seq'), None, 'tp'), parts along dimension 0, may hold values from -6 to 6
- decode_value_cache: bfloat16 [64, 256, 4, 128], P(('groups', 'seq'), None, 'tp'), parts along dimension 0, may hold values from -6 to 6
- owner_map: int32 [32, 1], P('groups'), parts along dimension 0, may hold values from 0 to 7; in each aligned block of 16 rows (0 to 15, 16 to 31, ...) at most 4 rows name the same one
- decode_lengths: int32 [32], P('groups'), parts along dimension 0, may hold values from 1 to 256
Outputs:
- prefill_out: bfloat16 [128, 64, 128], P(('groups', 'seq'), 'tp'), parts along dimension 0
- decode_out: bfloat16 [64, 64, 128], P(('groups', 'seq'), 'tp'), parts along dimension 0
There are 2 independent parts, one for each index of `groups`. A program takes and returns all parts, laid end to end along the dimension named above; each array names one. Nothing has to cross between parts.
Inputs may be any that keep to these rules, and one draw needn't show every extreme that they name: `owner_map`: no shard owns more than 4 requests, and some shard owns exactly 4.
All inputs are finite; a program needn't handle non-finite values.
Results may differ from a plain program's by a relative error of at most 0.005.
Values may be sent and summed in bfloat16 or wider, within the bound.
A program may use at most 64 MiB of HBM per device.

v0:
```python
import jax
import jax.numpy as jnp
from jax import lax
from jax.sharding import PartitionSpec as P

LOWEST = -1e30


def lookup_small(table, wanted):
    columns = jnp.arange(table.shape[0], dtype=jnp.int32)
    return jnp.sum(jnp.where(wanted[:, None] == columns[None, :], table[None, :], 0), axis=1)


def block_split(length):
    blocks = 1
    while length // blocks > 512 or length % blocks != 0:
        blocks += 1
    return blocks


def online_step(carried, queries, key_rows, value_rows, allowed):
    running_max, normalizer, weighted = carried
    scale = queries.shape[-1] ** (-0.5)
    scores = (
        jnp.einsum("tkgd,nkd->tkgn", queries, key_rows, preferred_element_type=jnp.float32) * scale
    )
    visible = allowed[:, None, None, :]
    scores = jnp.where(visible, scores, LOWEST)
    new_max = jnp.maximum(running_max, jnp.max(scores, axis=-1))
    weights = jnp.where(visible, jnp.exp(scores - new_max[..., None]), 0.0)
    factor = jnp.exp(running_max - new_max)
    normalizer = normalizer * factor + jnp.sum(weights, axis=-1)
    weighted = weighted * factor[..., None] + jnp.einsum(
        "tkgn,nkd->tkgd",
        weights.astype(jnp.bfloat16),
        value_rows,
        preferred_element_type=jnp.float32,
    )
    return (new_max, normalizer, weighted)


def guarded_step(carried, queries, key_rows, value_rows, allowed):
    return lax.cond(
        jnp.any(allowed),
        lambda inner: online_step(inner, queries, key_rows, value_rows, allowed),
        lambda inner: inner,
        carried,
    )


def fold_rows(carried, queries, key_rows, value_rows, allowed):
    length = key_rows.shape[0]
    blocks = block_split(length)
    if blocks == 1:
        return guarded_step(carried, queries, key_rows, value_rows, allowed)
    width = length // blocks
    stacked = (
        key_rows.reshape((blocks, width) + key_rows.shape[1:]),
        value_rows.reshape((blocks, width) + value_rows.shape[1:]),
        allowed.reshape(allowed.shape[0], blocks, width).transpose(1, 0, 2),
    )

    def visit(inner_carry, parts):
        return (guarded_step(inner_carry, queries, parts[0], parts[1], parts[2]), None)

    carried, unused = lax.scan(visit, carried, stacked)
    return carried


def on_device(
    span_queries,
    span_keys,
    span_values,
    prefix_keys,
    prefix_values,
    prefix_lengths,
    decode_queries,
    decode_new_keys,
    decode_new_values,
    decode_key_cache,
    decode_value_cache,
    owner_map,
    decode_lengths,
):
    device = lax.axis_index("seq")
    tokens_here, heads_here, head_dim = span_queries.shape
    kv_here = span_keys.shape[1]
    group_size = heads_here // kv_here
    queries = span_queries.reshape(tokens_here, kv_here, group_size, head_dim)
    token_index = device * tokens_here + jnp.arange(tokens_here, dtype=jnp.int32)
    prefix_here = prefix_keys.shape[0]
    initial = (
        jnp.full((tokens_here, kv_here, group_size), LOWEST, jnp.float32),
        jnp.zeros((tokens_here, kv_here, group_size), jnp.float32),
        jnp.zeros((tokens_here, kv_here, group_size, head_dim), jnp.float32),
    )
    stride = prefix_here + tokens_here
    both_keys = jnp.concatenate([prefix_keys, span_keys], axis=0)
    both_values = jnp.concatenate([prefix_values, span_values], axis=0)
    carried = initial
    key_rows = lax.all_gather(both_keys, "seq", axis=0, tiled=True)
    value_rows = lax.all_gather(both_values, "seq", axis=0, tiled=True)
    length = key_rows.shape[0]
    shards = length // stride
    tail = key_rows.shape[1:]
    keys_split = key_rows.reshape((shards, stride) + tail)
    values_split = value_rows.reshape((shards, stride) + tail)
    prefix_k = keys_split[:, :prefix_here].reshape((shards * prefix_here,) + tail)
    prefix_v = values_split[:, :prefix_here].reshape((shards * prefix_here,) + tail)
    span_k = keys_split[:, prefix_here:].reshape((shards * tokens_here,) + tail)
    span_v = values_split[:, prefix_here:].reshape((shards * tokens_here,) + tail)
    prefix_position = jnp.arange(shards * prefix_here, dtype=jnp.int32)
    prefix_ok = prefix_position % prefix_here < lookup_small(
        prefix_lengths, prefix_position // prefix_here
    )
    carried = fold_rows(
        carried,
        queries,
        prefix_k,
        prefix_v,
        jnp.broadcast_to(prefix_ok[None, :], (tokens_here, prefix_k.shape[0])),
    )
    span_position = jnp.arange(shards * tokens_here, dtype=jnp.int32)
    carried = fold_rows(
        carried, queries, span_k, span_v, span_position[None, :] <= token_index[:, None]
    )
    running_max, normalizer, weighted = carried
    prefill_out = (
        (weighted / normalizer[..., None])
        .reshape(tokens_here, heads_here, head_dim)
        .astype(jnp.bfloat16)
    )
    owners = owner_map[:, 0]
    requests = owners.shape[0]
    order = jnp.arange(requests, dtype=jnp.int32)
    earlier = (owners[None, :] == owners[:, None]) & (order[None, :] < order[:, None])
    ranking = jnp.sum(earlier.astype(jnp.int32), axis=1)
    slots_here = decode_key_cache.shape[0]
    slot_ids = jnp.arange(slots_here, dtype=jnp.int32)
    query_rows = lax.all_gather(decode_queries, "seq", axis=0, tiled=True)
    new_keys = lax.all_gather(decode_new_keys, "seq", axis=0, tiled=True)
    new_values = lax.all_gather(decode_new_values, "seq", axis=0, tiled=True)
    chosen = (owners == device)[None, :] & (ranking[None, :] == slot_ids[:, None])
    selector = chosen.astype(jnp.bfloat16)
    picked_queries = jnp.einsum(
        "sn,nhd->shd", selector, query_rows, preferred_element_type=jnp.float32
    )
    picked_keys = jnp.einsum("sn,nkd->skd", selector, new_keys, preferred_element_type=jnp.float32)
    picked_values = jnp.einsum(
        "sn,nkd->skd", selector, new_values, preferred_element_type=jnp.float32
    )
    picked_lengths = jnp.sum(jnp.where(chosen, decode_lengths[None, :], 0), axis=1)
    context = decode_key_cache.shape[1]
    grouped = picked_queries.astype(jnp.bfloat16).reshape(slots_here, kv_here, group_size, head_dim)
    own_keys = picked_keys.astype(jnp.bfloat16)
    own_values = picked_values.astype(jnp.bfloat16)
    scale = head_dim ** (-0.5)
    scores = (
        jnp.einsum("skgd,sckd->skgc", grouped, decode_key_cache, preferred_element_type=jnp.float32)
        * scale
    )
    visible = (jnp.arange(context, dtype=jnp.int32)[None, :] < picked_lengths[:, None])[
        :, None, None, :
    ]
    scores = jnp.where(visible, scores, LOWEST)
    own_score = (
        jnp.einsum("skgd,skd->skg", grouped, own_keys, preferred_element_type=jnp.float32) * scale
    )
    top_score = jnp.maximum(jnp.max(scores, axis=-1), own_score)
    weights = jnp.where(visible, jnp.exp(scores - top_score[..., None]), 0.0)
    own_weight = jnp.exp(own_score - top_score)
    total_weight = jnp.sum(weights, axis=-1) + own_weight
    rounded_own = lax.optimization_barrier(own_weight.astype(jnp.bfloat16)).astype(jnp.float32)
    mixed = jnp.einsum(
        "skgc,sckd->skgd",
        weights.astype(jnp.bfloat16),
        decode_value_cache,
        preferred_element_type=jnp.float32,
    )
    mixed = mixed + rounded_own[..., None] * own_values.astype(jnp.float32)[:, :, None, :]
    count_here = jnp.sum((owners == device).astype(jnp.int32))
    used = (slot_ids < count_here)[:, None, None, None]
    decode_out = (
        jnp.where(used, mixed / total_weight[..., None], 0.0)
        .reshape(slots_here, heads_here, head_dim)
        .astype(jnp.bfloat16)
    )
    return (prefill_out, decode_out)


def solution(mesh):
    return jax.shard_map(
        on_device,
        mesh=mesh,
        in_specs=(
            P(("groups", "seq"), "tp", None),
            P(("groups", "seq"), "tp", None),
            P(("groups", "seq"), "tp", None),
            P(("groups", "seq"), "tp", None),
            P(("groups", "seq"), "tp", None),
            P("groups"),
            P(("groups", "seq"), "tp", None),
            P(("groups", "seq"), "tp", None),
            P(("groups", "seq"), "tp", None),
            P(("groups", "seq"), None, "tp", None),
            P(("groups", "seq"), None, "tp", None),
            P("groups", None),
            P("groups"),
        ),
        out_specs=(P(("groups", "seq"), "tp", None), P(("groups", "seq"), "tp", None)),
        check_vma=False,
    )
```

profile of v0, /device:TPU:0, one launch (start us, length us, event | category | flops | bytes accessed | tf_op | source)
XLA Modules:
  0.0 148.8 jit_solution(11207647977653412298)
XLA Ops:
  0.7 0.7 iota_compare_fusion.3
  2.0 0.7 select_reduce_fusion
  2.9 0.7 copy-done.5
  3.6 32.7 %all_gather.15 = bf16[640,2,128]{2,1,0:T(2,128)(2,1)S(1)} all-gather(bf16[80,2,128]{2,1,0:T(2,128)(2,1)S(1)} %pad_maximum_fusion), channel_id=1, replica_groups=mesh['groups'=2,'seq'=8,'tp'=2] {'seq'}, dimensions={0}, use_global_device_ids=true | all-gather | bytes 368640 | tf_op jit(solution)/shard_map/all_gather | solution.py:101
  36.4 0.8 copy-done.1
  37.2 0.8 copy-done.3
  38.1 30.9 %all_gather.16 = bf16[640,2,128]{2,1,0:T(2,128)(2,1)S(1)} all-gather(bf16[80,2,128]{2,1,0:T(2,128)(2,1)S(1)} %pad_maximum_fusion.1), channel_id=1, replica_groups=mesh['groups'=2,'seq'=8,'tp'=2] {'seq'}, dimensions={0}, use_global_device_ids=true | all-gather | bytes 368640 | tf_op jit(solution)/shard_map/all_gather | solution.py:102
  69.1 4.4 %while.14 = (s32[]{:T(128)}, f32[8,2,16]{2,0,1:T(8,128)S(1)}, f32[8,2,16]{2,0,1:T(8,128)S(1)}, f32[8,2,16,128]{3,2,0,1:T(8,128)S(1)}, pred[2,8,288]{2,1,0:T(8,12...) while((s32[]{:T(128)}, f32[8,2,16]{2,0,1:T(8,128)S(1)}, ...), condition=%wide.region_8.9_spmd, body=%wide.region_2.8_spmd.sunk | while | flops 38480640 | bytes 1649647 | solution.py:66
  69.2 0.7 fusion.72
  70.5 0.9 conditional.4
  70.5 0.3 fusion.67
  70.8 0.2 fusion.4
  71.1 0.3 fusion.2
  71.4 0.7 fusion.72
  72.7 0.9 conditional.4
  72.7 0.3 fusion.67
  73.3 0.3 fusion.2
  73.6 0.7 conditional.2
  73.6 0.3 fusion.68
  74.1 0.2 fusion.16
  74.5 0.6 copy.71
  75.2 30.5 %all_gather.17 = bf16[16,32,128]{2,1,0:T(8,128)(2,1)S(1)} all-gather(bf16[2,32,128]{2,1,0:T(8,128)(2,1)S(1)} %copy-done.4), channel_id=1, replica_groups=mesh['groups'=2,'seq'=8,'tp'=2] {'seq'}, dimensions={0}, use_global_device_ids=true | all-gather | bytes 147456 | tf_op jit(solution)/shard_map/all_gather | solution.py:140
  105.7 0.7 copy-done.10
  106.5 0.6 convert_reduce_fusion.1
  107.2 0.7 copy-done.9
  108.2 0.3 fusion.69
  108.5 0.7 copy-done.7
  109.2 20.5 %all_gather.18 = bf16[16,2,128]{2,1,0:T(2,128)(2,1)S(1)} all-gather(bf16[2,2,128]{2,1,0:T(2,128)(2,1)S(1)} %copy-done.7), channel_id=1, replica_groups=mesh['groups'=2,'seq'=8,'tp'=2] {'seq'}, dimensions={0}, use_global_device_ids=true | all-gather | bytes 9216 | tf_op jit(solution)/shard_map/all_gather | solution.py:141
  130.2 0.7 copy-done.8
  130.8 16.3 %all_gather.19 = bf16[16,2,128]{2,1,0:T(2,128)(2,1)S(1)} all-gather(bf16[2,2,128]{2,1,0:T(2,128)(2,1)S(1)} %copy-done.8), channel_id=1, replica_groups=mesh['groups'=2,'seq'=8,'tp'=2] {'seq'}, dimensions={0}, use_global_device_ids=true | all-gather | bytes 9216 | tf_op jit(solution)/shard_map/all_gather | solution.py:142
  147.2 0.6 iota_compare_fusion.5
  147.9 0.9 fusion.34
  (57 shorter events, 2.2 us)
Async XLA Ops:
  0.6 107.6 %copy-start = (bf16[4,256,2,128]{3,2,1,0:T(2,128)(2,1)S(1)}, bf16[4,256,2,128]{3,2,1,0:T(2,128)(2,1)}, u32[]{:S(2)}) copy-start(bf16[4,256,2,128]{3,2,1,0:T(2,128)(2,1)} %param.28) | copy-start | bytes 1572868
  0.6 2.3 %copy-start.2 = (bf16[72,2,128]{2,1,0:T(2,128)(2,1)S(1)}, bf16[72,2,128]{2,1,0:T(2,128)(2,1)}, u32[]{:S(2)}) copy-start(bf16[72,2,128]{2,1,0:T(2,128)(2,1)} %param.22) | copy-start | bytes 110596
  2.9 0.7 copy-start.5
  36.4 0.8 copy-start.1
  37.2 0.8 copy-start.3
  37.2 0.8 copy-start.6
  74.5 0.7 copy-start.4
  105.7 0.7 copy-start.10
  107.2 0.7 copy-start.9
  108.1 39.8 %copy-start.11 = (bf16[4,256,2,128]{3,2,1,0:T(2,128)(2,1)S(1)}, bf16[4,256,2,128]{3,2,1,0:T(2,128)(2,1)}, u32[]{:S(2)}) copy-start(bf16[4,256,2,128]{3,2,1,0:T(2,128)(2,1)} %param.29) | copy-start | bytes 1572868
  108.5 0.7 copy-start.7
  130.1 0.7 copy-start.8
where the time goes:
time: 149 us
  blocking collectives  131 us (88%)
  local copies, waits for them, and re-layouts  5.93 us (4%)
  other arithmetic  5.57 us (4%)
  matrix products  3.39 us (2%)
  between operations  1.53 us (1%)
  loops' own time  1.5 us (1%)
    all_gather x1, blocking collectives, on_device(): key_rows = lax.all_gather(both_keys, 'seq', axis=0, tiled=True)  32.7 us
    all_gather x1, blocking collectives, on_device(): value_rows = lax.all_gather(both_values, 'seq', axis=0, tiled=True)  30.9 us
    all_gather x1, blocking collectives, on_device(): query_rows = lax.all_gather(decode_queries, 'seq', axis=0, tiled=True)  30.5 us
    all_gather x1, blocking collectives, on_device(): new_keys = lax.all_gather(decode_new_keys, 'seq', axis=0, tiled=True)  20.5 us
    all_gather x1, blocking collectives, on_device(): new_values = lax.all_gather(decode_new_values, 'seq', axis=0, tiled=True)  16.3 us
    unnamed x24, local copies, waits for them, and re-layouts  4.99 us

commit v1 on v0

v1 whole, which is shorter than its diff:
```python
import functools
import math

import jax
import jax.numpy as jnp
from jax import lax
from jax.experimental import pallas as pl
from jax.experimental.pallas import tpu as pltpu
from jax.sharding import PartitionSpec as P

LOWEST = -1e30
MESH = pl.DeviceIdType.MESH
NT = (((1,), (1,)), ((), ()))
TN = (((0,), (0,)), ((), ()))
NN = (((1,), (0,)), ((), ()))
KEYS, VALUES, QUERIES, NEW = range(4)


def repeat(low, high, body, carry, unrolled):
    if unrolled:
        for step in range(low, high):
            carry = body(step, carry)
        return carry
    return lax.fori_loop(low, high, body, carry)


def kernel(
    n,
    tokens,
    heads,
    kv,
    span_q,
    span_k,
    span_v,
    prefix_k,
    prefix_v,
    prefix_len,
    dec_q,
    new_k,
    new_v,
    cache_k,
    cache_v,
    owner,
    dec_len,
    out_prefill,
    out_decode,
    q_buf,
    k_buf,
    v_buf,
    dq_buf,
    new_buf,
    ck_buf,
    cv_buf,
    plen,
    own,
    dlen,
    local_sem,
    send_sem,
    recv_sem,
):
    me = lax.axis_index("seq")
    group = heads // kv
    prefix_rows = prefix_k.shape[0]
    span_rows = span_k.shape[0]
    here = dec_q.shape[0]
    requests = own.shape[0]
    slots = cache_k.shape[0]
    factor = q_buf.shape[-1] ** (-0.5) * math.log2(math.e)
    half = (n + 1) // 2
    small = n <= 16

    odd = me % 2
    place = (1 - odd) * (me // 2) + odd * (n - 1 - me // 2)

    def index_at(spot):
        spot = lax.rem(spot + 2 * n, n)
        upper = (spot >= half).astype(jnp.int32) if not isinstance(spot, int) else int(spot >= half)
        return (1 - upper) * (2 * spot) + upper * (2 * (n - 1 - spot) + 1)

    right, left = index_at(place + 1), index_at(place - 1)

    locals_ = [
        pltpu.make_async_copy(source, target, local_sem.at[at])
        for at, (source, target) in enumerate(
            (
                (dec_q, dq_buf.at[pl.ds(me * here, here)]),
                (new_k, new_buf.at[me, 0]),
                (new_v, new_buf.at[me, 1]),
                (prefix_k, k_buf.at[me, pl.ds(0, prefix_rows)]),
                (span_k, k_buf.at[me, pl.ds(prefix_rows, span_rows)]),
                (prefix_v, v_buf.at[me, pl.ds(0, prefix_rows)]),
                (span_v, v_buf.at[me, pl.ds(prefix_rows, span_rows)]),
                (span_q, q_buf),
                (prefix_len, plen),
                (owner, own),
                (dec_len, dlen),
                (cache_k, ck_buf),
                (cache_v, cv_buf),
            )
        )
    ]
    barrier = pltpu.get_barrier_semaphore()
    for neighbour in (left, right):
        pl.semaphore_signal(barrier, inc=1, device_id={"seq": neighbour}, device_id_type=MESH)
    for copy in locals_:
        copy.start()
    pl.semaphore_wait(barrier, 2)

    def part(kind, index):
        if kind == KEYS:
            return k_buf.at[index]
        if kind == VALUES:
            return v_buf.at[index]
        if kind == QUERIES:
            return dq_buf.at[pl.ds(index * here, here)]
        return new_buf.at[index]

    def message(way, step, kind, arriving=False):
        sign = 1 if way == 0 else -1
        index = index_at(place - sign * (step + (1 if arriving else 0)))
        return pltpu.make_async_remote_copy(
            src_ref=part(kind, index),
            dst_ref=part(kind, index),
            send_sem=send_sem.at[way, step, kind],
            recv_sem=recv_sem.at[way, step, kind],
            device_id={"seq": right if way == 0 else left},
            device_id_type=MESH,
        )

    full = (n - 1) // 2
    split = n % 2 == 0
    kinds_of_split = ((QUERIES, KEYS), (NEW, VALUES))
    order = (QUERIES, NEW, KEYS, VALUES)

    def send(step, kinds):
        for kind in kinds:
            for way in (0, 1):
                message(way, step, kind).start()

    def send_last(kinds):
        for way in (0, 1):
            for kind in kinds_of_split[way]:
                if kind in kinds:
                    message(way, full, kind).start()

    def dispatch(step, kinds):
        if full == 0:
            send_last(kinds)
        else:
            send(step, kinds)

    locals_[0].wait()
    dispatch(0, (QUERIES,))
    locals_[1].wait()
    locals_[2].wait()
    dispatch(0, (NEW,))
    locals_[3].wait()
    locals_[4].wait()
    dispatch(0, (KEYS,))
    locals_[5].wait()
    locals_[6].wait()
    dispatch(0, (VALUES,))
    locals_[7].wait()
    locals_[8].wait()

    rows = prefix_rows + span_rows
    lanes = q_buf.shape[0]
    row = lax.broadcasted_iota(jnp.int32, (rows, lanes), 0)
    lane = lax.broadcasted_iota(jnp.int32, (rows, lanes), 1)
    match = (row % kv) == (lane % heads) // group
    query_time = jnp.where(match, me * tokens + lane // heads, -1)
    in_prefix = row < prefix_rows
    span_time = (row - prefix_rows) // kv

    def attend(shard, carry):
        top, total, mixed = carry
        scores = lax.dot_general(
            k_buf[shard], q_buf[...], NT, preferred_element_type=jnp.float32
        )
        key_time = jnp.where(
            in_prefix,
            jnp.where(row < plen[shard] * kv, 0, n * tokens),
            span_time + shard * tokens,
        )
        scores = jnp.where(key_time <= query_time, scores, LOWEST)
        new_top = jnp.maximum(top, jnp.max(scores, axis=0, keepdims=True))
        weights = jnp.exp2((scores - new_top) * factor)
        decay = jnp.exp2((top - new_top) * factor)
        total = total * decay + jnp.sum(weights, axis=0, keepdims=True)
        mixed = mixed * decay + lax.dot_general(
            v_buf[shard], weights.astype(jnp.bfloat16), TN, preferred_element_type=jnp.float32
        )
        return new_top, total, mixed

    carry = (
        jnp.full((1, lanes), LOWEST, jnp.float32),
        jnp.zeros((1, lanes), jnp.float32),
        jnp.zeros((q_buf.shape[1], lanes), jnp.float32),
    )
    carry = attend(me, carry)

    def arrive(step, kinds, forward):
        for kind in kinds:
            for way in (0, 1):
                message(way, step, kind, True).wait_recv()
                if forward == "full":
                    message(way, step + 1, kind).start()
                elif forward == "split" and kind in kinds_of_split[way]:
                    message(way, full, kind).start()

    def ring_step(step, carry):
        arrive(step, order, "full")
        carry = attend(index_at(place - step - 1), carry)
        return attend(index_at(place + step + 1), carry)

    carry = repeat(0, full - 1, ring_step, carry, small)
    if full >= 1:
        arrive(full - 1, order, "split" if split else None)
        carry = attend(index_at(place - full), carry)
        carry = attend(index_at(place + full), carry)
    if split:
        message(0, full, QUERIES, True).wait_recv()
        message(1, full, NEW, True).wait_recv()

    for copy in locals_[9:]:
        copy.wait()

    def find(request, found):
        count, picks = found
        mine = own[request] == me
        picks = tuple(
            jnp.where(mine & (count == slot), request, pick) for slot, pick in enumerate(picks)
        )
        return count + jnp.where(mine, 1, 0), picks

    count, picks = repeat(
        0, requests, find, (jnp.int32(0), tuple(jnp.int32(0) for _ in range(slots))), small
    )
    cols = ck_buf.shape[1]
    head = lax.broadcasted_iota(jnp.int32, (heads, cols), 0)
    col = lax.broadcasted_iota(jnp.int32, (heads, cols), 1)
    bound = jnp.where(col % kv == head // group, col, cols)

    def spread(pair):
        pair = pair.astype(jnp.float32)
        return jnp.concatenate(
            [jnp.broadcast_to(pair[j : j + 1], (group, pair.shape[1])) for j in range(kv)], axis=0
        )

    for slot in range(slots):
        pick = picks[slot]
        queries = dq_buf[pick]
        own_key = spread(new_buf[pick // here, 0, pick % here])
        own_value = spread(new_buf[pick // here, 1, pick % here])
        scores = lax.dot_general(queries, ck_buf[slot], NT, preferred_element_type=jnp.float32)
        scores = jnp.where(bound < dlen[pick] * kv, scores, LOWEST)
        own_score = jnp.sum(queries.astype(jnp.float32) * own_key, axis=1, keepdims=True)
        top = jnp.maximum(jnp.max(scores, axis=1, keepdims=True), own_score)
        weights = jnp.exp2((scores - top) * factor)
        own_weight = jnp.exp2((own_score - top) * factor)
        total = jnp.sum(weights, axis=1, keepdims=True) + own_weight
        mixed = lax.dot_general(
            weights.astype(jnp.bfloat16), cv_buf[slot], NN, preferred_element_type=jnp.float32
        )
        mixed = mixed + own_weight.astype(jnp.bfloat16).astype(jnp.float32) * own_value
        result = jnp.where(slot < count, mixed / total, 0.0)
        out_decode[slot] = result.astype(out_decode.dtype)

    if split:
        message(0, full, KEYS, True).wait_recv()
        message(1, full, VALUES, True).wait_recv()
        carry = attend(index_at(place + full + 1), carry)
    top, total, mixed = carry
    out_prefill[...] = (mixed / total).T.astype(out_prefill.dtype)

    def finish(step, unused):
        for kind in order:
            for way in (0, 1):
                message(way, step, kind).wait_send()
        return unused

    repeat(0, full, finish, 0, small)
    if split:
        for way in (0, 1):
            for kind in kinds_of_split[way]:
                message(way, full, kind).wait_send()


def on_device(
    n,
    span_queries,
    span_keys,
    span_values,
    prefix_keys,
    prefix_values,
    prefix_lengths,
    decode_queries,
    decode_new_keys,
    decode_new_values,
    decode_key_cache,
    decode_value_cache,
    owner_map,
    decode_lengths,
):
    tokens, heads, dim = span_queries.shape
    kv = span_keys.shape[1]
    slots, context = decode_key_cache.shape[:2]
    here = decode_queries.shape[0]
    requests = owner_map.shape[0]
    rows = (prefix_keys.shape[0] + tokens) * kv
    steps = max(1, n // 2)
    bf16 = jnp.bfloat16
    any_space = pl.BlockSpec(memory_space=pl.ANY)
    vmem = pl.BlockSpec(memory_space=pltpu.VMEM)
    prefill, decode = pl.pallas_call(
        functools.partial(kernel, n, tokens, heads, kv),
        out_shape=(
            jax.ShapeDtypeStruct((tokens * heads, dim), bf16),
            jax.ShapeDtypeStruct((slots, heads, dim), bf16),
        ),
        in_specs=[any_space] * 13,
        out_specs=(vmem, vmem),
        scratch_shapes=[
            pltpu.VMEM((tokens * heads, dim), bf16),
            pltpu.VMEM((n, rows, dim), bf16),
            pltpu.VMEM((n, rows, dim), bf16),
            pltpu.VMEM((requests, heads, dim), bf16),
            pltpu.VMEM((n, 2, here, kv, dim), bf16),
            pltpu.VMEM((slots, context * kv, dim), bf16),
            pltpu.VMEM((slots, context * kv, dim), bf16),
            pltpu.SMEM(prefix_lengths.shape, jnp.int32),
            pltpu.SMEM((requests,), jnp.int32),
            pltpu.SMEM(decode_lengths.shape, jnp.int32),
            pltpu.SemaphoreType.DMA((13,)),
            pltpu.SemaphoreType.DMA((2, steps, 4)),
            pltpu.SemaphoreType.DMA((2, steps, 4)),
        ],
        compiler_params=pltpu.CompilerParams(collective_id=0, has_side_effects=True),
        name="mixed_attention",
    )(
        span_queries.reshape(tokens * heads, dim),
        span_keys.reshape(tokens * kv, dim),
        span_values.reshape(tokens * kv, dim),
        prefix_keys.reshape(-1, dim),
        prefix_values.reshape(-1, dim),
        prefix_lengths,
        decode_queries,
        decode_new_keys,
        decode_new_values,
        decode_key_cache.reshape(slots, context * kv, dim),
        decode_value_cache.reshape(slots, context * kv, dim),
        owner_map.reshape(requests),
        decode_lengths,
    )
    return prefill.reshape(tokens, heads, dim), decode


def solution(mesh):
    rows = P(("groups", "seq"), "tp", None)
    cache = P(("groups", "seq"), None, "tp", None)
    return jax.shard_map(
        functools.partial(on_device, mesh.shape["seq"]),
        mesh=mesh,
        in_specs=(
            rows,
            rows,
            rows,
            rows,
            rows,
            P("groups"),
            rows,
            rows,
            rows,
            cache,
            cache,
            P("groups", None),
            P("groups"),
        ),
        out_specs=(rows, rows),
        check_vma=False,
    )
```

time: 149 us -> 22.8 us (0.15)
  blocking collectives: 131 us -> 0 us
  Pallas kernels: 0 us -> 19.9 us
  other arithmetic: 5.57 us -> 0 us
  local copies, waits for them, and re-layouts: 5.93 us -> 2.1 us
  matrix products: 3.39 us -> 0 us
  loops' own time: 1.5 us -> 0 us
    all_gather x5 -> x0, blocking collectives: 131 us -> none  [the longest x1 32.7 us: on_device(): key_rows = lax.all_gather(both_keys, 'seq', axis=0, tiled=True)]
    pallas_call x0 -> x1, Pallas kernels: none -> 19.9 us  [on_device(): pl.pallas_call(functools.partial(kernel, n, tokens, heads, kv), out_shape...]
    dot_general x12 -> x0, matrix products: 3.39 us -> none  [the longest x1 0.87 us: on_device(): jnp.einsum('skgc,sckd->skgd', weights.astype(jnp.bfloat16), decode_value_...]
    unnamed x24 -> x4, local copies, waits for them, and re-layouts: 4.99 us -> 2.1 us
    reduce_sum x8 -> x0, other arithmetic: 2.48 us -> none  [the longest x1 0.74 us: lookup_small(): jnp.sum(jnp.where(wanted[:, None] == columns[None, :], table[None, :], 0)...]
    another operation x4 -> x0, loops' own time: 1.5 us -> none  [the longest x1 1.33 us: fold_rows(): carried, unused = lax.scan(visit, carried, stacked)]
where the time goes in v1:
time: 22.8 us; the launch traced here: 22.7 us
  Pallas kernels  19.9 us (87%)
  local copies, waits for them, and re-layouts  2.1 us (9%)
  between operations  0.65 us (3%)
    pallas_call x1, Pallas kernels, on_device(): pl.pallas_call(functools.partial(kernel, n, tokens, heads, kv), out_shape...  19.9 us
    unnamed x4, local copies, waits for them, and re-layouts  2.1 us

profile of v1, /device:TPU:0, one launch (start us, length us, event | category | flops | bytes accessed | tf_op | source)
XLA Modules:
  0.0 22.7 jit_solution(17399912125734124592)
XLA Ops:
  0.6 19.9 %mixed_attention.1 = (bf16[256,128]{1,0:T(8,128)(2,1)}, bf16[4,32,128]{2,1,0:T(8,128)(2,1)}) custom-call(bf16[256,128]{1,0:T(8,128)(2,1)} %bitcast.11, bf16[16,128]{1,0:T(8,128)(2,1)} %bitcast.15, bf16[16,128]{1,0:T(8,128)(2,1)} %bitcast.16, bf16[144,128]{1,0:T(8,128)(2,1)} %bitcast.13, bf16[144,128]{1,0:T(8,128)(2,1)} %bitcast.14, s32[8]{0:T(128)} %prefix_len.1, ...), custom_call_target="tpu_custom_call" | custom-call | tf_op jit(solution)/shard_map/mixed_attention/pallas_call | solution.py:315
  20.6 0.0 copy-start
  20.6 1.5 %copy.17 = bf16[8,32,128]{2,1,0:T(8,128)(2,1)} copy(bf16[8,32,128]{2,1,0:T(8,128)(2,1)} %bitcast.12) | data formatting | bytes 131072
  22.1 0.0 copy-done
  22.1 0.6 %copy.18 = bf16[4,32,128]{2,1,0:T(8,128)(2,1)} copy(bf16[4,32,128]{2,1,0:T(8,128)(2,1)S(1)} %copy-done) | data formatting | bytes 65536
Async XLA Ops:
  20.6 1.5 %copy-start = (bf16[4,32,128]{2,1,0:T(8,128)(2,1)S(1)}, bf16[4,32,128]{2,1,0:T(8,128)(2,1)}, u32[]{:S(2)}) copy-start(bf16[4,32,128]{2,1,0:T(8,128)(2,1)} %get-tuple-element.9) | copy-start | bytes 98308

commit v2 on v1

--- a/solution.py
+++ b/solution.py
@@ -315,8 +315,8 @@
     prefill, decode = pl.pallas_call(
         functools.partial(kernel, n, tokens, heads, kv),
         out_shape=(
-            jax.ShapeDtypeStruct((tokens * heads, dim), bf16),
-            jax.ShapeDtypeStruct((slots, heads, dim), bf16),
+            pltpu.VMEM((tokens * heads, dim), bf16),
+            pltpu.VMEM((slots, heads, dim), bf16),
         ),
         in_specs=[any_space] * 13,
         out_specs=(vmem, vmem),

time: 22.8 us -> 21.4 us (0.939)
  local copies, waits for them, and re-layouts: 2.1 us -> 1.25 us
  Pallas kernels: 19.9 us -> 19.3 us
    unnamed x4 -> x2, local copies, waits for them, and re-layouts: 2.1 us -> 1.25 us
    pallas_call x1, Pallas kernels: 19.9 us -> 19.3 us  [on_device(): pl.pallas_call(functools.partial(kernel, n, tokens, heads, kv), out_shape...]
where the time goes in v2:
time: 21.4 us; the launch traced here: 21.2 us
  Pallas kernels  19.3 us (90%)
  local copies, waits for them, and re-layouts  1.25 us (6%)
  between operations  0.64 us (3%)
    pallas_call x1, Pallas kernels, on_device(): pl.pallas_call(functools.partial(kernel, n, tokens, heads, kv), out_shape...  19.3 us
    unnamed x2, local copies, waits for them, and re-layouts  1.25 us

profile of v2, /device:TPU:0, one launch (start us, length us, event | category | flops | bytes accessed | tf_op | source)
XLA Modules:
  0.0 21.2 jit_solution(1358609783939826992)
XLA Ops:
  0.6 19.3 %mixed_attention.1 = (bf16[256,128]{1,0:T(8,128)(2,1)S(1)}, bf16[4,32,128]{2,1,0:T(8,128)(2,1)S(1)}) custom-call(bf16[256,128]{1,0:T(8,128)(2,1)} %bitcast.12, bf16[16,128]{1,0:T(8,128)(2,1)} %bitcast.15, bf16[16,128]{1,0:T(8,128)(2,1)} %bitcast.16, bf16[144,128]{1,0:T(8,128)(2,1)} %bitcast.13, bf16[144,128]{1,0:T(8,128)(2,1)} %bitcast.14, s32[8]{0:T(128)} %prefix_len.1, ...), custom_call_target="tpu_custom_call" | custom-call | tf_op jit(solution)/shard_map/mixed_attention/pallas_call | solution.py:315
  19.9 0.6 %copy.17 = bf16[8,32,128]{2,1,0:T(8,128)(2,1)} copy(bf16[8,32,128]{2,1,0:T(8,128)(2,1)S(1)} %bitcast.9) | data formatting | bytes 131072
  20.6 0.6 %copy.18 = bf16[4,32,128]{2,1,0:T(8,128)(2,1)} copy(bf16[4,32,128]{2,1,0:T(8,128)(2,1)S(1)} %get-tuple-element.7) | data formatting | bytes 65536

commit v3 on v2

--- a/solution.py
+++ b/solution.py
@@ -14,6 +14,7 @@
 TN = (((0,), (0,)), ((), ()))
 NN = (((1,), (0,)), ((), ()))
 KEYS, VALUES, QUERIES, NEW = range(4)
+ACROSS, ALONG, RELAY = range(3)
 
 
 def repeat(low, high, body, carry, unrolled):
@@ -69,15 +70,21 @@
     half = (n + 1) // 2
     small = n <= 16
 
-    odd = me % 2
-    place = (1 - odd) * (me // 2) + odd * (n - 1 - me // 2)
-
-    def index_at(spot):
-        spot = lax.rem(spot + 2 * n, n)
-        upper = (spot >= half).astype(jnp.int32) if not isinstance(spot, int) else int(spot >= half)
-        return (1 - upper) * (2 * spot) + upper * (2 * (n - 1 - spot) + 1)
-
-    right, left = index_at(place + 1), index_at(place - 1)
+    depth = n // 2
+    chip, column = me // 2, me % 2
+    partner = 2 * chip + 1 - column
+    paired = depth & (depth - 1) == 0
+    relayed = depth == 4
+    inner = (chip % 3 + 1) // 2 if relayed else 0
+
+    def hop(turn, back=False):
+        if not paired:
+            return 2 * lax.rem(chip + (depth - turn if back else turn), depth) + column
+        spot = 0
+        for bit in range(depth.bit_length() - 1):
+            own_bit, turn_bit = (chip // 2**bit) % 2, (turn // 2**bit) % 2
+            spot = spot + 2**bit * (own_bit + turn_bit - 2 * own_bit * turn_bit)
+        return 2 * spot + column
 
     locals_ = [
         pltpu.make_async_copy(source, target, local_sem.at[at])
@@ -100,11 +107,22 @@
         )
     ]
     barrier = pltpu.get_barrier_semaphore()
-    for neighbour in (left, right):
-        pl.semaphore_signal(barrier, inc=1, device_id={"seq": neighbour}, device_id_type=MESH)
+
+    def hello(target):
+        pl.semaphore_signal(barrier, inc=1, device_id={"seq": target}, device_id_type=MESH)
+
+    def greet(turn, unused):
+        if relayed and turn == 3:
+            pl.when(inner == 1)(lambda: hello(hop(turn)))
+        else:
+            hello(hop(turn))
+        return unused
+
+    hello(partner)
+    repeat(1, depth, greet, 0, small)
     for copy in locals_:
         copy.start()
-    pl.semaphore_wait(barrier, 2)
+    pl.semaphore_wait(barrier, depth - 1 + inner if relayed else depth)
 
     def part(kind, index):
         if kind == KEYS:
@@ -115,51 +133,63 @@
             return dq_buf.at[pl.ds(index * here, here)]
         return new_buf.at[index]
 
-    def message(way, step, kind, arriving=False):
-        sign = 1 if way == 0 else -1
-        index = index_at(place - sign * (step + (1 if arriving else 0)))
+    def message(role, turn, kind, index, target):
         return pltpu.make_async_remote_copy(
             src_ref=part(kind, index),
             dst_ref=part(kind, index),
-            send_sem=send_sem.at[way, step, kind],
-            recv_sem=recv_sem.at[way, step, kind],
-            device_id={"seq": right if way == 0 else left},
+            send_sem=send_sem.at[role, turn, kind],
+            recv_sem=recv_sem.at[index, kind],
+            device_id={"seq": target},
             device_id_type=MESH,
         )
 
-    full = (n - 1) // 2
-    split = n % 2 == 0
-    kinds_of_split = ((QUERIES, KEYS), (NEW, VALUES))
+    def arrived(kind, index):
+        message(ACROSS, 0, kind, index, partner).wait_recv()
+
     order = (QUERIES, NEW, KEYS, VALUES)
 
-    def send(step, kinds):
-        for kind in kinds:
-            for way in (0, 1):
-                message(way, step, kind).start()
-
-    def send_last(kinds):
-        for way in (0, 1):
-            for kind in kinds_of_split[way]:
-                if kind in kinds:
-                    message(way, full, kind).start()
-
-    def dispatch(step, kinds):
-        if full == 0:
-            send_last(kinds)
+    def along(turn, kind, action):
+        copy = message(ALONG, turn, kind, me, hop(turn))
+        if relayed and turn == 3:
+            pl.when(inner == 1)(lambda: action(copy))
         else:
-            send(step, kinds)
+            action(copy)
+
+    def relay(turn, kind, action):
+        if relayed:
+            copy = message(RELAY, 0, kind, hop(2), hop(1))
+            pl.when((inner == 1) & (turn == 2))(lambda: action(copy))
+
+    def start(copy):
+        copy.start()
+
+    def finish_send(copy):
+        copy.wait_send()
+
+    def dispatch(kind):
+        message(ACROSS, 0, kind, me, partner).start()
+
+        def go(turn, unused):
+            along(turn, kind, start)
+            return unused
+
+        if relayed:
+            for turn in (2, 3, 1):
+                go(turn, 0)
+        else:
+            repeat(1, depth, go, 0, small)
 
     locals_[0].wait()
-    dispatch(0, (QUERIES,))
+    dispatch(QUERIES)
     locals_[1].wait()
     locals_[2].wait()
-    dispatch(0, (NEW,))
+    dispatch(NEW)
     locals_[3].wait()
     locals_[4].wait()
-    dispatch(0, (KEYS,))
+    dispatch(KEYS)
     locals_[5].wait()
     locals_[6].wait()
-    dispatch(0, (VALUES,))
+    dispatch(VALUES)
     locals_[7].wait()
     locals_[8].wait()
 
@@ -199,29 +229,50 @@
     )
     carry = attend(me, carry)
 
-    def arrive(step, kinds, forward):
-        for kind in kinds:
-            for way in (0, 1):
-                message(way, step, kind, True).wait_recv()
-                if forward == "full":
-                    message(way, step + 1, kind).start()
-                elif forward == "split" and kind in kinds_of_split[way]:
-                    message(way, full, kind).start()
-
-    def ring_step(step, carry):
-        arrive(step, order, "full")
-        carry = attend(index_at(place - step - 1), carry)
-        return attend(index_at(place + step + 1), carry)
-
-    carry = repeat(0, full - 1, ring_step, carry, small)
-    if full >= 1:
-        arrive(full - 1, order, "split" if split else None)
-        carry = attend(index_at(place - full), carry)
-        carry = attend(index_at(place + full), carry)
-    if split:
-        message(0, full, QUERIES, True).wait_recv()
-        message(1, full, NEW, True).wait_recv()
-
+    def turn_at(step):
+        if not relayed:
+            return step + 1
+        return (1 + inner, 2 + inner, 3 - 2 * inner)[step]
+
+    def pass_on(step, kind):
+        turn = turn_at(step)
+        source = hop(turn, True)
+        arrived(kind, source)
+        relay(turn, kind, start)
+        message(ACROSS, turn, kind, source, partner).start()
+        return source
+
+    def pass_all(kind):
+        def go(step, unused):
+            pass_on(step, kind)
+            return unused
+
+        repeat(0, depth - 1, go, 0, small)
+
+    pass_all(QUERIES)
+    pass_all(NEW)
+    pass_all(KEYS)
+    arrived(KEYS, partner)
+    arrived(VALUES, partner)
+    carry = attend(partner, carry)
+
+    def take(step, carry):
+        return attend(pass_on(step, VALUES), carry)
+
+    carry = repeat(0, depth - 1, take, carry, small)
+
+    def other(source):
+        return source + 1 - 2 * column
+
+    arrived(QUERIES, partner)
+    arrived(NEW, partner)
+
+    def settle(step, unused):
+        arrived(QUERIES, other(hop(turn_at(step), True)))
+        arrived(NEW, other(hop(turn_at(step), True)))
+        return unused
+
+    repeat(0, depth - 1, settle, 0, small)
     for copy in locals_[9:]:
         copy.wait()
 
@@ -266,24 +317,37 @@
         result = jnp.where(slot < count, mixed / total, 0.0)
         out_decode[slot] = result.astype(out_decode.dtype)
 
-    if split:
-        message(0, full, KEYS, True).wait_recv()
-        message(1, full, VALUES, True).wait_recv()
-        carry = attend(index_at(place + full + 1), carry)
+    def close(step, carry):
+        source = other(hop(turn_at(step), True))
+        arrived(KEYS, source)
+        arrived(VALUES, source)
+        return attend(source, carry)
+
+    carry = repeat(0, depth - 1, close, carry, small)
     top, total, mixed = carry
     out_prefill[...] = (mixed / total).T.astype(out_prefill.dtype)
 
-    def finish(step, unused):
-        for kind in order:
-            for way in (0, 1):
-                message(way, step, kind).wait_send()
-        return unused
-
-    repeat(0, full, finish, 0, small)
-    if split:
-        for way in (0, 1):
-            for kind in kinds_of_split[way]:
-                message(way, full, kind).wait_send()
+    for kind in order:
+        message(ACROSS, 0, kind, me, partner).wait_send()
+        relay(2, kind, finish_send)
+
+        def finish(turn, unused):
+            along(turn, kind, finish_send)
+            message(ACROSS, turn, kind, hop(turn, True), partner).wait_send()
+            return unused
+
+        repeat(1, depth, finish, 0, small)
+
+
+def store(prefill, decode, out_prefill, out_decode, sem):
+    copies = (
+        pltpu.make_async_copy(prefill, out_prefill, sem.at[0]),
+        pltpu.make_async_copy(decode, out_decode, sem.at[1]),
+    )
+    for copy in copies:
+        copy.start()
+    for copy in copies:
+        copy.wait()
 
 
 def on_device(
@@ -308,7 +372,6 @@
     here = decode_queries.shape[0]
     requests = owner_map.shape[0]
     rows = (prefix_keys.shape[0] + tokens) * kv
-    steps = max(1, n // 2)
     bf16 = jnp.bfloat16
     any_space = pl.BlockSpec(memory_space=pl.ANY)
     vmem = pl.BlockSpec(memory_space=pltpu.VMEM)
@@ -332,8 +395,8 @@
             pltpu.SMEM((requests,), jnp.int32),
             pltpu.SMEM(decode_lengths.shape, jnp.int32),
             pltpu.SemaphoreType.DMA((13,)),
-            pltpu.SemaphoreType.DMA((2, steps, 4)),
-            pltpu.SemaphoreType.DMA((2, steps, 4)),
+            pltpu.SemaphoreType.DMA((3, n // 2, 4)),
+            pltpu.SemaphoreType.DMA((n, 4)),
         ],
         compiler_params=pltpu.CompilerParams(collective_id=0, has_side_effects=True),
         name="mixed_attention",
@@ -352,6 +415,17 @@
         owner_map.reshape(requests),
         decode_lengths,
     )
+    prefill, decode = pl.pallas_call(
+        store,
+        out_shape=(
+            jax.ShapeDtypeStruct((tokens * heads, dim), bf16),
+            jax.ShapeDtypeStruct((slots, heads, dim), bf16),
+        ),
+        in_specs=[vmem, vmem],
+        out_specs=[any_space, any_space],
+        scratch_shapes=[pltpu.SemaphoreType.DMA((2,))],
+        name="store_outputs",
+    )(*(pltpu.with_memory_space_constraint(x, pltpu.VMEM) for x in (prefill, decode)))
     return prefill.reshape(tokens, heads, dim), decode
 
 

time: 21.4 us -> 20.7 us (0.967)
  local copies, waits for them, and re-layouts: 1.25 us -> 0 us
  Pallas kernels: 19.3 us -> 19.9 us
    unnamed x2 -> x0, local copies, waits for them, and re-layouts: 1.25 us -> none
    pallas_call x0 -> x1, Pallas kernels: none -> 0.66 us  [on_device(): pl.pallas_call(store, out_shape=(jax.ShapeDtypeStruct((tokens * heads, di...]
where the time goes in v3:
time: 20.7 us; the launch traced here: 20.5 us
  Pallas kernels  19.9 us (96%)
  between operations  0.64 us (3%)
    pallas_call x1, Pallas kernels, on_device(): pl.pallas_call(functools.partial(kernel, n, tokens, heads, kv), out_shape...  19.2 us
    pallas_call x1, Pallas kernels, on_device(): pl.pallas_call(store, out_shape=(jax.ShapeDtypeStruct((tokens * heads, di...  0.66 us

profile of v3, /device:TPU:0, one launch (start us, length us, event | category | flops | bytes accessed | tf_op | source)
XLA Modules:
  0.0 20.5 jit_solution(9757603819463102632)
XLA Ops:
  0.6 19.2 %mixed_attention.1 = (bf16[256,128]{1,0:T(8,128)(2,1)S(1)}, bf16[4,32,128]{2,1,0:T(8,128)(2,1)S(1)}) custom-call(bf16[256,128]{1,0:T(8,128)(2,1)} %bitcast.11, bf16[16,128]{1,0:T(8,128)(2,1)} %bitcast.14, bf16[16,128]{1,0:T(8,128)(2,1)} %bitcast.15, bf16[144,128]{1,0:T(8,128)(2,1)} %bitcast.12, bf16[144,128]{1,0:T(8,128)(2,1)} %bitcast.13, s32[8]{0:T(128)} %prefix_len.1, ...), custom_call_target="tpu_custom_call" | custom-call | tf_op jit(solution)/shard_map/mixed_attention/pallas_call | solution.py:378
  19.8 0.7 %store_outputs.1 = (bf16[256,128]{1,0:T(8,128)(2,1)}, bf16[4,32,128]{2,1,0:T(8,128)(2,1)}) custom-call(bf16[256,128]{1,0:T(8,128)(2,1)S(1)} %get-tuple-element.6.prefill, bf16[4,32,128]{2,1,0:T(8,128)(2,1)S(1)} %get-tuple-element.7.decode), custom_call_target="tpu_custom_call" | custom-call | tf_op jit(solution)/shard_map/store_outputs/pallas_call | solution.py:418
